TPU v7x, 32 devices: a whole 2x2x4 slice. The times are simulated.
32 devices in a mesh: slab: 8 (over z, core), split: 4 (over y, x).
Axes of the slice: x: 2, y: 2, z: 4, core: 2. Of those that a mesh axis runs over, the one named last changes fastest.
Arguments:
- displacement: float32 [3, 64, 128, 256], P(None, 'slab', 'split'), may hold values from -0.3 to 0.3
- velocity: float32 [3, 64, 128, 256], P(None, 'slab', 'split'), may hold values from -0.6 to 0.6
- acceleration: float32 [3, 64, 128, 256], P(None, 'slab', 'split'), may hold values from -1.8 to 1.8
- bond_masks: int32 [4, 64, 128, 256], P(None, 'slab', 'split'), may hold values from 0 to 255, as said below
- proj_pos: float32 [32, 3, 128], replicated, may hold values from -0.5 to 257, as said below
- proj_vel: float32 [32, 3, 128], replicated, may hold values from -1.8 to 1.8
- proj_acc: float32 [32, 3, 128], replicated, may hold values from -1.8 to 1.8
- contact_pairs: int32 [3, 2, 512], P(None, None, ('slab', 'split')), may hold values from -1 to 31, as said below
Outputs:
- final_displacement: float32 [3, 64, 128, 256], P(None, 'slab', 'split')
- final_velocity: float32 [3, 64, 128, 256], P(None, 'slab', 'split')
- final_proj_pos: float32 [32, 3, 128], replicated
- final_proj_vel: float32 [32, 3, 128], replicated
Inputs may be any that keep to these rules, and one draw needn't show every extreme that they name: `bond_masks`: bit b of word w (the value divided by 2 to the b, modulo 2) is 1 where the bond from the cell to the offset numbered 8 w + b is intact. `contact_pairs`: slots d * 16 to (d + 1) * 16 - 1 belong to device d. Row 0 names one of that device's 8 surface blocks; row 1 names a projectile block, or -1 for an empty slot. Live slots come first on every device and no pair repeats on a device within a substep. In every substep each projectile block is paired on exactly one device, one of the four devices of the 2 x 2 group of device blocks under it, and on another device than in the substep before; in every substep some device has all 16 slots live. `proj_pos`: the device blocks fall into 2 x 2 groups (slab indices 2a and 2a + 1, split indices 2b and 2b + 1). Every projectile block lies above one such group, between 0.5 and 2 cells over the top layer, and every group lies under exactly 4 projectile blocks.
All inputs are finite; a program needn't handle non-finite values.
Results may differ from a plain program's by a relative error of at most 0.0003.
Values sent between devices are 32-bit elements; how exact they have to be, the bound alone decides.
A program may use at most 128 MiB of HBM per device.

v0:
```python
import math

import jax
import jax.numpy as jnp
from jax import lax
from jax.sharding import PartitionSpec as P

SUB = 3
SL = 4
PTS = 128
SB_DEV = 8


time_step = 0.25
bond_stiffness = 0.5
contact_stiffness = 0.05
contact_width = 8.0
inverse_mass = 0.5


def with_halo(cells, sides, width):
    for axis, dim in sides:
        count = lax.axis_size(axis)
        ends = count - 1
        head = lax.slice_in_dim(cells, 0, width, axis=dim)
        tail = lax.slice_in_dim(cells, cells.shape[dim] - width, cells.shape[dim], axis=dim)
        cells = jnp.concatenate(
            [
                lax.ppermute(tail, axis, [(i, (i + 1) % count) for i in range(ends)]),
                cells,
                lax.ppermute(head, axis, [((i + 1) % count, i) for i in range(ends)]),
            ],
            axis=dim,
        )
    return cells


def bond_offsets():
    listed = []
    for shift_x in (-2, -1, 0, 1, 2):
        for shift_y in (-2, -1, 0, 1, 2):
            for shift_z in (-2, -1, 0, 1, 2):
                squared = shift_x * shift_x + shift_y * shift_y + shift_z * shift_z
                if 0 < squared <= 4:
                    listed.append((shift_x, shift_y, shift_z))
    return listed


def bond_term(neighbour, displace, intact, valid_bond, offset):
    shift_x, shift_y, shift_z = offset
    length = math.sqrt(shift_x * shift_x + shift_y * shift_y + shift_z * shift_z)
    along_x = shift_x + (neighbour[0] - displace[0])
    along_y = shift_y + (neighbour[1] - displace[1])
    along_z = shift_z + (neighbour[2] - displace[2])
    squared = along_x * along_x + along_y * along_y + along_z * along_z
    stretch = (squared - length * length) / (length * (jnp.sqrt(squared) + length))
    return bond_stiffness / length * stretch * intact * valid_bond


def add_bond(bond_total, coefficient, offset):
    direction = jnp.array(offset, bond_total.dtype)
    return bond_total + direction[:, None, None, None] * coefficient[None]


def shift_depth(values_in, shift_size):
    if shift_size == 0:
        return values_in
    filler = jnp.zeros(values_in.shape[:-1] + (abs(shift_size),), values_in.dtype)
    if shift_size > 0:
        return jnp.concatenate([values_in[..., shift_size:], filler], axis=-1)
    return jnp.concatenate([filler, values_in[..., :shift_size]], axis=-1)


def bond_forces(padded, displace, mask_words, inside_x, inside_y):
    cells_x, cells_y, cells_z = (displace.shape[1], displace.shape[2], displace.shape[3])
    depth_index = jnp.arange(cells_z)
    bond_total = jnp.zeros_like(displace)
    for number, offset in enumerate(bond_offsets()):
        shift_x, shift_y, shift_z = offset
        window = padded[
            :, 2 + shift_x : 2 + shift_x + cells_x, 2 + shift_y : 2 + shift_y + cells_y, :
        ]
        neighbour = shift_depth(window, shift_z)
        moved_depth = depth_index + shift_z
        inside_z = ((moved_depth >= 0) & (moved_depth < cells_z)).astype(jnp.float32)
        valid_bond = (
            inside_x[2 + shift_x : 2 + shift_x + cells_x][:, None, None]
            * inside_y[2 + shift_y : 2 + shift_y + cells_y][None, :, None]
            * inside_z[None, None, :]
        )
        intact = (mask_words[number // 8] // 2 ** (number % 8) % 2).astype(jnp.float32)
        bond_total = add_bond(
            bond_total, bond_term(neighbour, displace, intact, valid_bond, offset), offset
        )
    return bond_total


def contact_tile(points, particles):
    separation = points[:, :, None] - particles[:, None, :]
    squared = jnp.sum(separation * separation, axis=0)
    weight = contact_stiffness * jnp.exp(-squared / contact_width)
    pulled = weight[None] * separation
    return (jnp.sum(pulled, axis=2), -jnp.sum(pulled, axis=1))


def slot_tiles(slot_points, chosen, positions):
    picked = positions[jnp.maximum(chosen, 0)]
    on_points, on_particles = jax.vmap(contact_tile)(slot_points, picked)
    live = (chosen >= 0).astype(jnp.float32)[:, None, None]
    return (on_points * live, on_particles * live)


def per_device(
    displacement, velocity, acceleration, bond_masks, proj_pos, proj_vel, proj_acc, contact_pairs
):
    cells_x, cells_y, cells_z = (
        displacement.shape[1],
        displacement.shape[2],
        displacement.shape[3],
    )
    slab_count = lax.axis_size("slab")
    split_count = lax.axis_size("split")
    corner_x = lax.axis_index("slab") * cells_x
    corner_y = lax.axis_index("split") * cells_y
    span_x = jnp.arange(-2, cells_x + 2) + corner_x
    span_y = jnp.arange(-2, cells_y + 2) + corner_y
    inside_x = ((span_x >= 0) & (span_x < slab_count * cells_x)).astype(jnp.float32)
    inside_y = ((span_y >= 0) & (span_y < split_count * cells_y)).astype(jnp.float32)
    place_x = (corner_x + jnp.arange(cells_x)).astype(jnp.float32)
    place_y = (corner_y + jnp.arange(cells_y)).astype(jnp.float32)
    place_z = (cells_z - SL + jnp.arange(SL)).astype(jnp.float32)
    lattice = jnp.stack(
        [
            jnp.broadcast_to(place_x[:, None, None], (cells_x, cells_y, SL)),
            jnp.broadcast_to(place_y[None, :, None], (cells_x, cells_y, SL)),
            jnp.broadcast_to(place_z[None, None, :], (cells_x, cells_y, SL)),
        ]
    )
    blocks_total = proj_pos.shape[0]
    particle_slots = jnp.arange(blocks_total)
    block_slots = jnp.arange(SB_DEV)
    for substep in range(SUB):
        half_velocity = velocity + 0.5 * time_step * acceleration
        displacement = displacement + time_step * half_velocity
        proj_half = proj_vel + 0.5 * time_step * proj_acc
        proj_pos = proj_pos + time_step * proj_half
        padded = with_halo(displacement, (("slab", 1), ("split", 2)), 2)
        forces = bond_forces(padded, displacement, bond_masks, inside_x, inside_y)
        top_layers = displacement[:, :, :, cells_z - SL :]
        places = (top_layers + lattice).reshape(3, SB_DEV, PTS)
        slot_pairs = contact_pairs[substep]
        targets = slot_pairs[0]
        chosen = slot_pairs[1]
        slot_points = jnp.moveaxis(jnp.take(places, targets, axis=1), 1, 0)
        on_points, on_particles = slot_tiles(slot_points, chosen, proj_pos)
        target_hits = (targets[:, None] == block_slots[None, :]).astype(jnp.float32)
        surface = jnp.einsum("ks,kcp->csp", target_hits, on_points, precision=lax.Precision.HIGHEST)
        forces = forces + jnp.pad(
            surface.reshape(3, cells_x, cells_y, SL), ((0, 0), (0, 0), (0, 0), (cells_z - SL, 0))
        )
        particle_hits = (chosen[:, None] == particle_slots[None, :]).astype(jnp.float32)
        particle_local = jnp.einsum(
            "kb,kcp->bcp", particle_hits, on_particles, precision=lax.Precision.HIGHEST
        )
        acceleration = forces
        velocity = half_velocity + 0.5 * time_step * acceleration
        particle_force = lax.psum(particle_local, ("slab", "split"))
        proj_acc = inverse_mass * particle_force
        proj_vel = proj_half + 0.5 * time_step * proj_acc
    return (displacement, velocity, proj_pos, proj_vel)


def solution(mesh):
    placed = (
        P(None, "slab", "split", None),
        P(None, "slab", "split", None),
        P(None, "slab", "split", None),
        P(None, "slab", "split", None),
        P(),
        P(),
        P(),
        P(None, None, ("slab", "split")),
    )
    return jax.shard_map(
        per_device,
        mesh=mesh,
        in_specs=placed,
        out_specs=(P(None, "slab", "split", None), P(None, "slab", "split", None), P(), P()),
        check_vma=False,
    )
```

profile of v0, /device:TPU:4, one launch (start us, length us, event | category | flops | bytes accessed | tf_op | source)
XLA Modules:
  0.0 279.7 jit_solution(2510947669306366044)
XLA Ops:
  0.6 1.8 multiply_add_fusion.3
  4.5 3.0 %collective-permute-start = (f32[3,2,32,256]{3,2,1,0:T(8,128)S(1)}, f32[3,2,32,256]{3,2,1,0:T(8,128)S(1)}, u32[]{:S(2)}, u32[]{:S(2)}) collective-permute-start(f32[3,2,32,256]{3,2,1,0:T(8,128)S(1)} %get-tuple-element.217), channel_id=1, source_target_pairs={{0,4},{4,8},{8,12},{12,16},{16,20},{20,24},{24,28},{1,5},{5,9},{9,... | collective-permute-start | bytes 589832 | tf_op jit(solution)/shard_map/ppermute | solution.py:29
  10.4 1.4 fusion.1172
  15.8 2.0 fusion
  18.2 1.4 copy.483
  20.0 41.7 %psum.21 = f32[32,3,128]{2,0,1:T(8,128)S(1)} all-reduce(f32[32,3,128]{2,0,1:T(8,128)S(1)} %fusion.1136), channel_id=1, replica_groups=mesh['slab'=8,'split'=4] {'slab','split'}, use_global_device_ids=true, to_apply=%region_3.5 | all-reduce | flops 12288 | bytes 98304 | tf_op jit(solution)/shard_map/psum | solution.py:167
  65.6 3.3 %collective-permute-start.3 = (f32[3,12,2,256]{3,2,1,0:T(2,128)S(1)}, f32[3,12,2,256]{3,2,1,0:T(2,128)S(1)}, u32[]{:S(2)}, u32[]{:S(2)}) collective-permute-start(f32[3,12,2,256]{3,2,1,0:T(2,128)S(1)} %get-tuple-element.190), channel_id=1, source_target_pairs={{1,0},{2,1},{3,2},{5,4},{6,5},{7,6},{9,8},{10,9},{11,10},{13,12},{... | collective-permute-start | bytes 221192 | tf_op jit(solution)/shard_map/ppermute | solution.py:31
  69.0 2.8 collective-permute-start.2
  71.7 2.5 fusion.16
  76.4 2.9 %fusion.1166 = (f32[3,8,32,255]{3,2,1,0:T(8,128)S(1)}, f32[3,8,32,255]{3,2,1,0:T(8,128)S(1)}, f32[3,8,32,255]{3,2,1,0:T(8,128)S(1)}, f32[3,8,32,255]{3,2,1,0:T(8...) fusion(f32[3,12,34,256]{3,2,1,0:T(8,128)S(1)} %get-tuple-elemen, ...), kind=kLoop, calls=%fused_computation.1893 | loop fusion | bytes 18800640 | tf_op jit(solution)/shard_map/slice | solution.py:71
  79.3 1.9 fusion.102
  90.4 1.4 fusion.135
  99.2 3.3 %multiply_add_fusion.2 = (f32[3,8,32,256]{3,2,1,0:T(8,128)S(1)}, f32[3,8,32,256]{3,2,1,0:T(8,128)}) fusion(f32[3,8,32,256]{3,2,1,0:T(8,128)S(1)} %multiply_add_fusion.3, f32[3,8,32,4]{3,2,1,0:T(8,128)S(1)} %copy-done.17, f32[8,32,256]{2,1,0:T(8,128)S(1)} %get-tuple-element.69, f32[3]{0:T(128)S(1)} %copy-done.74, f32[8,32,256]{2,1,0:T(8,128)S(1)} %get-tuple-element.119, ...), kind=kLoop, calls=%fused_computation.134 | loop fusion | flops 13565952 | bytes 12333416 | tf_op jit(solution)/shard_map/add | solution.py:144
  106.3 2.7 fusion.2
  109.3 1.4 copy.491
  112.0 3.0 %collective-permute-start.4 = (f32[3,2,32,256]{3,2,1,0:T(8,128)}, f32[3,2,32,256]{3,2,1,0:T(8,128)S(1)}, u32[]{:S(2)}, u32[]{:S(2)}) collective-permute-start(f32[3,2,32,256]{3,2,1,0:T(8,128)} %get-tuple-element.210), channel_id=1, source_target_pairs={{0,4},{4,8},{8,12},{12,16},{16,20},{20,24},{24,28},{1,5},{5,9},{9,... | collective-permute-start | bytes 589832 | tf_op jit(solution)/shard_map/ppermute | solution.py:29
  116.1 41.0 %psum.22 = f32[32,3,128]{2,0,1:T(8,128)S(1)} all-reduce(f32[32,3,128]{2,0,1:T(8,128)S(1)} %fusion.1133), channel_id=1, replica_groups=mesh['slab'=8,'split'=4] {'slab','split'}, use_global_device_ids=true, to_apply=%region_7.9 | all-reduce | flops 12288 | bytes 98304 | tf_op jit(solution)/shard_map/psum | solution.py:167
  157.1 1.3 gather_fusion.2
  158.8 2.9 %collective-permute-start.6 = (f32[3,12,2,256]{3,2,1,0:T(2,128)S(1)}, f32[3,12,2,256]{3,2,1,0:T(2,128)S(1)}, u32[]{:S(2)}, u32[]{:S(2)}) collective-permute-start(f32[3,12,2,256]{3,2,1,0:T(2,128)S(1)} %get-tuple-element.186), channel_id=1, source_target_pairs={{0,1},{1,2},{2,3},{4,5},{5,6},{6,7},{8,9},{9,10},{10,11},{12,13},{... | collective-permute-start | bytes 221192 | tf_op jit(solution)/shard_map/ppermute | solution.py:29
  161.8 4.0 %collective-permute-start.7 = (f32[3,12,2,256]{3,2,1,0:T(2,128)S(1)}, f32[3,12,2,256]{3,2,1,0:T(2,128)S(1)}, u32[]{:S(2)}, u32[]{:S(2)}) collective-permute-start(f32[3,12,2,256]{3,2,1,0:T(2,128)S(1)} %get-tuple-element.187), channel_id=1, source_target_pairs={{1,0},{2,1},{3,2},{5,4},{6,5},{7,6},{9,8},{10,9},{11,10},{13,12},{... | collective-permute-start | bytes 221192 | tf_op jit(solution)/shard_map/ppermute | solution.py:31
  185.5 3.4 %multiply_add_fusion.1 = (f32[3,8,32,256]{3,2,1,0:T(8,128)S(1)}, f32[3,8,32,256]{3,2,1,0:T(8,128)}) fusion(f32[3,8,32,256]{3,2,1,0:T(8,128)S(1)} %get-tuple-element.31, f32[3,8,32,256]{3,2,1,0:T(8,128)S(1)} %copy-done.4, f32[3,8,32,4]{3,2,1,0:T(8,128)S(1)} %copy-done.18, f32[8,32,256]{2,1,0:T(8,128)S(1)} %get-tuple-element.67, f32[3]{0:T(128)S(1)} %copy-done.75, ...), kind=kLoop, calls=%fused_computation.133 | loop fusion | flops 13172736 | bytes 11546984 | tf_op jit(solution)/shard_map/add | solution.py:144
  191.8 1.3 copy.493
  195.6 1.8 fusion.8
  197.6 2.6 fusion.4
  200.6 1.4 copy.499
  203.2 3.0 %collective-permute-start.8 = (f32[3,2,32,256]{3,2,1,0:T(8,128)}, f32[3,2,32,256]{3,2,1,0:T(8,128)S(1)}, u32[]{:S(2)}, u32[]{:S(2)}) collective-permute-start(f32[3,2,32,256]{3,2,1,0:T(8,128)} %get-tuple-element.203), channel_id=1, source_target_pairs={{0,4},{4,8},{8,12},{12,16},{16,20},{20,24},{24,28},{1,5},{5,9},{9,... | collective-permute-start | bytes 589832 | tf_op jit(solution)/shard_map/ppermute | solution.py:29
  206.3 1.7 fusion.1130
  207.9 39.7 %psum.23 = f32[32,3,128]{2,0,1:T(8,128)} all-reduce(f32[32,3,128]{2,0,1:T(8,128)} %fusion.1130), channel_id=1, replica_groups=mesh['slab'=8,'split'=4] {'slab','split'}, use_global_device_ids=true, to_apply=%region_11.13 | all-reduce | flops 12288 | bytes 98304 | tf_op jit(solution)/shard_map/psum | solution.py:167
  247.6 1.5 multiply_add_fusion.5
  249.1 3.7 %collective-permute-start.10 = (f32[3,12,2,256]{3,2,1,0:T(2,128)S(1)}, f32[3,12,2,256]{3,2,1,0:T(2,128)S(1)}, u32[]{:S(2)}, u32[]{:S(2)}) collective-permute-start(f32[3,12,2,256]{3,2,1,0:T(2,128)S(1)} %get-tuple-element.182), channel_id=1, source_target_pairs={{0,1},{1,2},{2,3},{4,5},{5,6},{6,7},{8,9},{9,10},{10,11},{12,13},{... | collective-permute-start | bytes 221192 | tf_op jit(solution)/shard_map/ppermute | solution.py:29
  252.8 3.5 %collective-permute-start.11 = (f32[3,12,2,256]{3,2,1,0:T(2,128)S(1)}, f32[3,12,2,256]{3,2,1,0:T(2,128)S(1)}, u32[]{:S(2)}, u32[]{:S(2)}) collective-permute-start(f32[3,12,2,256]{3,2,1,0:T(2,128)S(1)} %get-tuple-element.183), channel_id=1, source_target_pairs={{1,0},{2,1},{3,2},{5,4},{6,5},{7,6},{9,8},{10,9},{11,10},{13,12},{... | collective-permute-start | bytes 221192 | tf_op jit(solution)/shard_map/ppermute | solution.py:31
  276.1 3.4 %multiply_add_fusion = f32[3,8,32,256]{3,2,1,0:T(8,128)} fusion(f32[3,8,32,256]{3,2,1,0:T(8,128)S(1)} %copy-done.3, f32[3,8,32,4]{3,2,1,0:T(8,128)S(1)} %copy-done.16, f32[8,32,256]{2,1,0:T(8,128)S(1)} %get-tuple-element.89, f32[8,32,256]{2,1,0:T(8,128)S(1)} %get-tuple-element.121, f32[8,32,256]{2,1,0:T(8,128)S(1)} %get-tuple-element.65, ...), kind=kLoop, calls=%fused_computation.132 | loop fusion | flops 12582912 | bytes 9974120 | tf_op jit(solution)/shard_map/add | solution.py:166
  (493 shorter events, 83.3 us)
Async XLA Ops:
  3.2 62.4 %collective-permute-start.1 = (f32[3,2,32,256]{3,2,1,0:T(8,128)}, f32[3,2,32,256]{3,2,1,0:T(8,128)S(1)}, u32[]{:S(2)}, u32[]{:S(2)}) collective-permute-start(f32[3,2,32,256]{3,2,1,0:T(8,128)} %get-tuple-element.218), channel_id=1, source_target_pairs={{4,0},{8,4},{12,8},{16,12},{20,16},{24,20},{28,24},{5,1},{9,5},{13... | collective-permute-start | bytes 589832 | tf_op jit(solution)/shard_map/ppermute | solution.py:31
  4.5 61.1 %collective-permute-start = (f32[3,2,32,256]{3,2,1,0:T(8,128)S(1)}, f32[3,2,32,256]{3,2,1,0:T(8,128)S(1)}, u32[]{:S(2)}, u32[]{:S(2)}) collective-permute-start(f32[3,2,32,256]{3,2,1,0:T(8,128)S(1)} %get-tuple-element.217), channel_id=1, source_target_pairs={{0,4},{4,8},{8,12},{12,16},{16,20},{20,24},{24,28},{1,5},{5,9},{9,... | collective-permute-start | bytes 589832 | tf_op jit(solution)/shard_map/ppermute | solution.py:29
  11.8 49.9 %copy-start.20 = (f32[32,3,128]{2,0,1:T(8,128)}, f32[32,3,128]{2,0,1:T(8,128)S(1)}, u32[]{:S(2)}) copy-start(f32[32,3,128]{2,0,1:T(8,128)S(1)} %multiply_add_fusion.8) | copy-start | bytes 147460
  15.8 46.6 %copy-start.166 = (s32[16]{0:T(128)S(1)}, s32[16]{0:T(128)}, u32[]{:S(2)}) copy-start(s32[16]{0:T(128)} %get-tuple-element.222) | copy-start | bytes 196
  15.8 46.6 %copy-start.168 = (s32[16]{0:T(128)S(1)}, s32[16]{0:T(128)}, u32[]{:S(2)}) copy-start(s32[16]{0:T(128)} %get-tuple-element.230) | copy-start | bytes 196
  15.8 47.2 %copy-start.165 = (s32[16]{0:T(128)S(1)}, s32[16]{0:T(128)}, u32[]{:S(2)}) copy-start(s32[16]{0:T(128)} %get-tuple-element.226) | copy-start | bytes 196
  15.8 47.8 %copy-start.167 = (s32[16]{0:T(128)S(1)}, s32[16]{0:T(128)}, u32[]{:S(2)}) copy-start(s32[16]{0:T(128)} %get-tuple-element.24) | copy-start | bytes 196
  65.5 13.8 %copy-start.59 = (f32[8,32]{1,0:T(8,128)}, f32[8,32]{1,0:T(8,128)S(1)}, u32[]{:S(2)}) copy-start(f32[8,32]{1,0:T(8,128)S(1)} %get-tuple-element.247) | copy-start | bytes 3076
  65.5 18.3 %copy-start.47 = (f32[8,32]{1,0:T(8,128)}, f32[8,32]{1,0:T(8,128)S(1)}, u32[]{:S(2)}) copy-start(f32[8,32]{1,0:T(8,128)S(1)} %get-tuple-element.242) | copy-start | bytes 3076
  65.5 21.9 %copy-start.41 = (f32[8,32]{1,0:T(8,128)}, f32[8,32]{1,0:T(8,128)S(1)}, u32[]{:S(2)}) copy-start(f32[8,32]{1,0:T(8,128)S(1)} %get-tuple-element.240) | copy-start | bytes 3076
  65.5 22.9 %copy-start.56 = (f32[8,32]{1,0:T(8,128)}, f32[8,32]{1,0:T(8,128)S(1)}, u32[]{:S(2)}) copy-start(f32[8,32]{1,0:T(8,128)S(1)} %get-tuple-element.245) | copy-start | bytes 3076
  65.5 23.9 %copy-start.35 = (f32[8,32]{1,0:T(8,128)}, f32[8,32]{1,0:T(8,128)S(1)}, u32[]{:S(2)}) copy-start(f32[8,32]{1,0:T(8,128)S(1)} %get-tuple-element.243) | copy-start | bytes 3076
  65.5 24.9 %copy-start.53 = (f32[8,32]{1,0:T(8,128)}, f32[8,32]{1,0:T(8,128)S(1)}, u32[]{:S(2)}) copy-start(f32[8,32]{1,0:T(8,128)S(1)} %get-tuple-element.237) | copy-start | bytes 3076
  65.5 26.3 %copy-start.32 = (f32[8,32]{1,0:T(8,128)}, f32[8,32]{1,0:T(8,128)S(1)}, u32[]{:S(2)}) copy-start(f32[8,32]{1,0:T(8,128)S(1)} %get-tuple-element.238) | copy-start | bytes 3076
  65.5 27.3 %copy-start.26 = (f32[8,32]{1,0:T(8,128)}, f32[8,32]{1,0:T(8,128)S(1)}, u32[]{:S(2)}) copy-start(f32[8,32]{1,0:T(8,128)S(1)} %get-tuple-element.236) | copy-start | bytes 3076
  65.5 28.6 %copy-start.38 = (f32[8,32]{1,0:T(8,128)}, f32[8,32]{1,0:T(8,128)S(1)}, u32[]{:S(2)}) copy-start(f32[8,32]{1,0:T(8,128)S(1)} %get-tuple-element.239) | copy-start | bytes 3076
  65.5 29.6 %copy-start.29 = (f32[8,32]{1,0:T(8,128)}, f32[8,32]{1,0:T(8,128)S(1)}, u32[]{:S(2)}) copy-start(f32[8,32]{1,0:T(8,128)S(1)} %get-tuple-element.244) | copy-start | bytes 3076
  65.5 30.7 %copy-start.62 = (f32[8,32]{1,0:T(8,128)}, f32[8,32]{1,0:T(8,128)S(1)}, u32[]{:S(2)}) copy-start(f32[8,32]{1,0:T(8,128)S(1)} %get-tuple-element.246) | copy-start | bytes 3076
  65.6 31.6 %copy-start.44 = (f32[8,32]{1,0:T(8,128)}, f32[8,32]{1,0:T(8,128)S(1)}, u32[]{:S(2)}) copy-start(f32[8,32]{1,0:T(8,128)S(1)} %get-tuple-element.235) | copy-start | bytes 3076
  65.6 9.8 %collective-permute-start.3 = (f32[3,12,2,256]{3,2,1,0:T(2,128)S(1)}, f32[3,12,2,256]{3,2,1,0:T(2,128)S(1)}, u32[]{:S(2)}, u32[]{:S(2)}) collective-permute-start(f32[3,12,2,256]{3,2,1,0:T(2,128)S(1)} %get-tuple-element.190), channel_id=1, source_target_pairs={{1,0},{2,1},{3,2},{5,4},{6,5},{7,6},{9,8},{10,9},{11,10},{13,12},{... | collective-permute-start | bytes 221192 | tf_op jit(solution)/shard_map/ppermute | solution.py:31
  69.0 7.1 %collective-permute-start.2 = (f32[3,12,2,256]{3,2,1,0:T(2,128)S(1)}, f32[3,12,2,256]{3,2,1,0:T(2,128)S(1)}, u32[]{:S(2)}, u32[]{:S(2)}) collective-permute-start(f32[3,12,2,256]{3,2,1,0:T(2,128)S(1)} %get-tuple-element.191), channel_id=1, source_target_pairs={{0,1},{1,2},{2,3},{4,5},{5,6},{6,7},{8,9},{9,10},{10,11},{12,13},{... | collective-permute-start | bytes 221192 | tf_op jit(solution)/shard_map/ppermute | solution.py:29
  106.3 50.8 %copy-start.21 = (f32[32,3,128]{2,0,1:T(8,128)S(1)}, f32[32,3,128]{2,0,1:T(8,128)}, u32[]{:S(2)}) copy-start(f32[32,3,128]{2,0,1:T(8,128)} %copy-done.20) | copy-start | bytes 147460
  106.3 50.8 %copy-start.22 = (f32[32,3,128]{2,0,1:T(8,128)S(1)}, f32[32,3,128]{2,0,1:T(8,128)}, u32[]{:S(2)}) copy-start(f32[32,3,128]{2,0,1:T(8,128)} %get-tuple-element.30) | copy-start | bytes 147460
  110.7 48.1 %collective-permute-start.5 = (f32[3,2,32,256]{3,2,1,0:T(8,128)}, f32[3,2,32,256]{3,2,1,0:T(8,128)S(1)}, u32[]{:S(2)}, u32[]{:S(2)}) collective-permute-start(f32[3,2,32,256]{3,2,1,0:T(8,128)} %get-tuple-element.211), channel_id=1, source_target_pairs={{4,0},{8,4},{12,8},{16,12},{20,16},{24,20},{28,24},{5,1},{9,5},{13... | collective-permute-start | bytes 589832 | tf_op jit(solution)/shard_map/ppermute | solution.py:31
  112.0 46.8 %collective-permute-start.4 = (f32[3,2,32,256]{3,2,1,0:T(8,128)}, f32[3,2,32,256]{3,2,1,0:T(8,128)S(1)}, u32[]{:S(2)}, u32[]{:S(2)}) collective-permute-start(f32[3,2,32,256]{3,2,1,0:T(8,128)} %get-tuple-element.210), channel_id=1, source_target_pairs={{0,4},{4,8},{8,12},{12,16},{16,20},{20,24},{24,28},{1,5},{5,9},{9,... | collective-permute-start | bytes 589832 | tf_op jit(solution)/shard_map/ppermute | solution.py:29
  158.8 13.7 %collective-permute-start.6 = (f32[3,12,2,256]{3,2,1,0:T(2,128)S(1)}, f32[3,12,2,256]{3,2,1,0:T(2,128)S(1)}, u32[]{:S(2)}, u32[]{:S(2)}) collective-permute-start(f32[3,12,2,256]{3,2,1,0:T(2,128)S(1)} %get-tuple-element.186), channel_id=1, source_target_pairs={{0,1},{1,2},{2,3},{4,5},{5,6},{6,7},{8,9},{9,10},{10,11},{12,13},{... | collective-permute-start | bytes 221192 | tf_op jit(solution)/shard_map/ppermute | solution.py:29
  161.8 10.8 %collective-permute-start.7 = (f32[3,12,2,256]{3,2,1,0:T(2,128)S(1)}, f32[3,12,2,256]{3,2,1,0:T(2,128)S(1)}, u32[]{:S(2)}, u32[]{:S(2)}) collective-permute-start(f32[3,12,2,256]{3,2,1,0:T(2,128)S(1)} %get-tuple-element.187), channel_id=1, source_target_pairs={{1,0},{2,1},{3,2},{5,4},{6,5},{7,6},{9,8},{10,9},{11,10},{13,12},{... | collective-permute-start | bytes 221192 | tf_op jit(solution)/shard_map/ppermute | solution.py:31
  188.9 85.5 %copy-start = (f32[3,8,32,256]{3,2,1,0:T(8,128)}, f32[3,8,32,256]{3,2,1,0:T(8,128)S(1)}, u32[]{:S(2)}) copy-start(f32[3,8,32,256]{3,2,1,0:T(8,128)S(1)} %get-tuple-element.25) | copy-start | bytes 2359300
  201.9 47.1 %collective-permute-start.9 = (f32[3,2,32,256]{3,2,1,0:T(8,128)}, f32[3,2,32,256]{3,2,1,0:T(8,128)S(1)}, u32[]{:S(2)}, u32[]{:S(2)}) collective-permute-start(f32[3,2,32,256]{3,2,1,0:T(8,128)} %get-tuple-element.204), channel_id=1, source_target_pairs={{4,0},{8,4},{12,8},{16,12},{20,16},{24,20},{28,24},{5,1},{9,5},{13... | collective-permute-start | bytes 589832 | tf_op jit(solution)/shard_map/ppermute | solution.py:31
  203.2 45.9 %collective-permute-start.8 = (f32[3,2,32,256]{3,2,1,0:T(8,128)}, f32[3,2,32,256]{3,2,1,0:T(8,128)S(1)}, u32[]{:S(2)}, u32[]{:S(2)}) collective-permute-start(f32[3,2,32,256]{3,2,1,0:T(8,128)} %get-tuple-element.203), channel_id=1, source_target_pairs={{0,4},{4,8},{8,12},{12,16},{16,20},{20,24},{24,28},{1,5},{5,9},{9,... | collective-permute-start | bytes 589832 | tf_op jit(solution)/shard_map/ppermute | solution.py:29
  249.1 14.1 %collective-permute-start.10 = (f32[3,12,2,256]{3,2,1,0:T(2,128)S(1)}, f32[3,12,2,256]{3,2,1,0:T(2,128)S(1)}, u32[]{:S(2)}, u32[]{:S(2)}) collective-permute-start(f32[3,12,2,256]{3,2,1,0:T(2,128)S(1)} %get-tuple-element.182), channel_id=1, source_target_pairs={{0,1},{1,2},{2,3},{4,5},{5,6},{6,7},{8,9},{9,10},{10,11},{12,13},{... | collective-permute-start | bytes 221192 | tf_op jit(solution)/shard_map/ppermute | solution.py:29
  252.8 10.4 %collective-permute-start.11 = (f32[3,12,2,256]{3,2,1,0:T(2,128)S(1)}, f32[3,12,2,256]{3,2,1,0:T(2,128)S(1)}, u32[]{:S(2)}, u32[]{:S(2)}) collective-permute-start(f32[3,12,2,256]{3,2,1,0:T(2,128)S(1)} %get-tuple-element.183), channel_id=1, source_target_pairs={{1,0},{2,1},{3,2},{5,4},{6,5},{7,6},{9,8},{10,9},{11,10},{13,12},{... | collective-permute-start | bytes 221192 | tf_op jit(solution)/shard_map/ppermute | solution.py:31
  (156 other events, 231.9 us)
where the time goes:
time: 285 us; the launch traced here: 280 us
  blocking collectives  122 us (43%)
  other arithmetic  86.6 us (30%)
  starting transfers between devices  33.1 us (12%)
  local copies, waits for them, and re-layouts  29.6 us (10%)
  between operations  3.84 us (1%)
  matrix products  3.58 us (1%)
    psum x3, blocking collectives, per_device(): particle_force = lax.psum(particle_local, ('slab', 'split'))  122 us
    mul x49, other arithmetic, add_bond(): return bond_total + direction[:, None, None, None] * coefficient[None]  47.4 us
    ppermute x6, starting transfers between devices, with_halo(): lax.ppermute(tail, axis, [(i, (i + 1) % count) for i in range(ends)])  18.5 us
    ppermute x6, starting transfers between devices, with_halo(): lax.ppermute(head, axis, [((i + 1) % count, i) for i in range(ends)])  14.6 us
    add x3, other arithmetic, per_device(): displacement = displacement + time_step * half_velocity  8.5 us
    slice x7, local copies, waits for them, and re-layouts, shift_depth(): return jnp.concatenate([filler, values_in[..., :shift_size]], axis=-1)  8.44 us
    reduce_sum x3, other arithmetic, contact_tile(): return (jnp.sum(pulled, axis=2), -jnp.sum(pulled, axis=1))  7.3 us
    concatenate x10, other arithmetic, with_halo(): jnp.concatenate([lax.ppermute(tail, axis, [(i, (i + 1) % count) for i in...  6.48 us
  transfers between devices with their start and end apart: 12, of which 1 were waited for; matrix products, arithmetic and copies ran while one was open for 14% of the time, Pallas kernels for 0%

commit v1 on v0

v1 whole, which is shorter than its diff:
```python
import functools
import math

import jax
import jax.numpy as jnp
from jax import lax
from jax.experimental import pallas as pl
from jax.experimental.pallas import tpu as pltpu
from jax.sharding import PartitionSpec as P

SL = 4
PTS = 128
SB_DEV = 8
LANES = 128

time_step = 0.25
bond_stiffness = 0.5
contact_stiffness = 0.05
contact_width = 8.0
inverse_mass = 0.5
tiny = 1e-30
MESH = pl.DeviceIdType.MESH


def bond_offsets():
    listed = []
    for shift_x in (-2, -1, 0, 1, 2):
        for shift_y in (-2, -1, 0, 1, 2):
            for shift_z in (-2, -1, 0, 1, 2):
                squared = shift_x * shift_x + shift_y * shift_y + shift_z * shift_z
                if 0 < squared <= 4:
                    listed.append((shift_x, shift_y, shift_z))
    return listed


OFFSETS = bond_offsets()
CORNERS = [(-1, -1), (-1, 1), (1, -1), (1, 1)]
SIDES = [(-1, 0), (1, 0), (0, -1), (0, 1)]


def kernel(
    dims,
    targets_ref, slots_ref, inverse_ref, mine_ref, place_ref,
    disp_ref, vel_ref, acc_ref, mask_ref, qpos_ref, qvel_ref, qacc_ref,
    out_disp, out_vel, out_pos, out_pvel,
    u_0, u_p, u_m, u_pp, u_mm, force, factors, edges_y, edges_c,
    got_x, got_y, got_c, wide, slot_point, slot_part, qp, qv, qa, rel,
    part_send, part_got, fin, gathered,
    send_x, recv_x, send_y, recv_y, send_c, recv_c, send_p, recv_p, send_g, recv_g,
):
    subs, nx, ny, nz, slabs, splits, per_group, blocks = dims
    halves = nz // LANES
    tiles = ny // 8
    slots = slots_ref.shape[0] // subs
    top = halves - 1
    me_x = lax.axis_index("slab")
    me_y = lax.axis_index("split")
    mid_x, mid_y = nx // 2, ny // 2
    half_split = splits // 2
    groups = (slabs // 2) * half_split
    my_group = (me_x // 2) * half_split + me_y // 2
    my_x, my_y = lax.rem(me_x, 2), lax.rem(me_y, 2)
    my_id = my_x * 2 + my_y

    def exists(dx, dy):
        ok = None
        for d, me, n in ((dx, me_x, slabs), (dy, me_y, splits)):
            if d:
                cond = (me > 0) if d < 0 else (me < n - 1)
                ok = cond if ok is None else ok & cond
        return ok

    barrier = pltpu.get_barrier_semaphore()

    def greet(x, y):
        pl.semaphore_signal(barrier, inc=1, device_id=(x, y), device_id_type=MESH)

    for dx, dy in SIDES + CORNERS:
        @pl.when(exists(dx, dy))
        def _():
            greet(me_x + dx, me_y + dy)

    def group_xy(g):
        return 2 * (g // half_split) + my_x, 2 * lax.rem(g, half_split) + my_y

    @pl.loop(0, groups)
    def _(g):
        @pl.when(g != my_group)
        def _():
            x, y = group_xy(g)
            greet(x, y)

    lane = lax.broadcasted_iota(jnp.int32, (8, LANES), 1)
    row8 = lax.broadcasted_iota(jnp.int32, (8, LANES), 0)

    zero_tile = jnp.zeros((8, LANES), jnp.float32)
    for ref in (u_0, u_p, u_m):
        for x in (0, 1, nx + 2, nx + 3):
            ref[:, x] = jnp.zeros(ref.shape[:1] + ref.shape[2:], jnp.float32)

        @pl.loop(2, nx + 2)
        def _(x):
            for c in range(3):
                for h in range(halves):
                    ref[c, x, h, 0:8, :] = zero_tile
                    ref[c, x, h, ny + 8 : ny + 16, :] = zero_tile

    @pl.loop(0, nx)
    def _(x):
        at_x = me_x * nx + x
        ok_x = {
            d: jnp.where((at_x + d >= 0) & (at_x + d < slabs * nx), 1.0, 0.0)
            for d in (-2, -1, 0, 1, 2)
        }
        for h in range(halves):
            at_z = lane + h * LANES
            ok_z = {d: (at_z + d >= 0) & (at_z + d < nz) for d in (-2, -1, 0, 1, 2)}
            for t in range(tiles):
                at_y = me_y * ny + t * 8 + row8
                ok_y = {
                    d: (at_y + d >= 0) & (at_y + d < splits * ny) for d in (-2, -1, 0, 1, 2)
                }
                words = [
                    mask_ref[w, x, t * 8 : t * 8 + 8, h * LANES : (h + 1) * LANES]
                    for w in range(4)
                ]
                for n, (dx, dy, dz) in enumerate(OFFSETS):
                    squared = dx * dx + dy * dy + dz * dz
                    scale = bond_stiffness / squared
                    if squared == 4:
                        scale = scale * 2.0
                    ok = ((words[n // 8] & (1 << (n % 8))) != 0) & ok_y[dy] & ok_z[dz]
                    factors[n, x, h, t * 8 : t * 8 + 8, :] = jnp.where(
                        ok, scale * ok_x[dx], 0.0
                    )
        for c in range(3):
            for h in range(halves):
                zs = slice(h * LANES, (h + 1) * LANES)
                out_vel[c, x, :, zs] = vel_ref[c, x, :, zs]
                out_disp[c, x, :, zs] = disp_ref[c, x, :, zs]
                force[c, x, h] = acc_ref[c, x, :, zs]

    for r in range(per_group):
        qp[r] = qpos_ref[mine_ref[r]]
        qv[r] = qvel_ref[mine_ref[r]]
        qa[r] = qacc_ref[mine_ref[r]]
    slot_point[slots] = jnp.zeros(slot_point.shape[1:], jnp.float32)
    slot_part[slots] = jnp.zeros(slot_part.shape[1:], jnp.float32)

    count = groups - 1
    for dx, dy in SIDES + CORNERS:
        count = count + jnp.where(exists(dx, dy), 1, 0)
    pl.semaphore_wait(barrier, count)

    def shifted(parts, by):
        rows = parts[0].shape[0]
        lanes = lax.broadcasted_iota(jnp.int32, (rows, LANES), 1)
        rolled = [pltpu.roll(p, (-by) % LANES, axis=1) for p in parts]
        out = []
        for h in range(len(parts)):
            other = h + 1 if by > 0 else h - 1
            if 0 <= other < len(parts):
                edge = lanes >= LANES - by if by > 0 else lanes < -by
                out.append(jnp.where(edge, rolled[other], rolled[h]))
            else:
                out.append(rolled[h])
        return out

    def put(c, x, rows, parts, shifts=True):
        for h, p in enumerate(parts):
            u_0[c, x, h, rows, :] = p
        if shifts:
            for ref, by in ((u_p, 1), (u_m, -1)):
                for h, p in enumerate(shifted(parts, by)):
                    ref[c, x, h, rows, :] = p + float(by) if c == 2 else p

    def copy_side(s, k, dx):
        src = u_0.at[:, 2:4, :, 8 : 8 + ny, :] if dx < 0 else u_0.at[:, nx : nx + 2, :, 8 : 8 + ny, :]
        return pltpu.make_async_remote_copy(
            src_ref=src, dst_ref=got_x.at[s, k], send_sem=send_x.at[s, k],
            recv_sem=recv_x.at[s, k], device_id=(me_x + dx, me_y), device_id_type=MESH,
        )

    def copy_edge(s, k, dy):
        return pltpu.make_async_remote_copy(
            src_ref=edges_y.at[s, k], dst_ref=got_y.at[s, k], send_sem=send_y.at[s, k],
            recv_sem=recv_y.at[s, k], device_id=(me_x, me_y + dy), device_id_type=MESH,
        )

    def copy_corner(s, k, dx, dy):
        return pltpu.make_async_remote_copy(
            src_ref=edges_c.at[s, k], dst_ref=got_c.at[s, k], send_sem=send_c.at[s, k],
            recv_sem=recv_c.at[s, k], device_id=(me_x + dx, me_y + dy), device_id_type=MESH,
        )

    def copy_part(s, p, flip_x, flip_y):
        px = me_x + (1 - 2 * my_x) * flip_x
        py = me_y + (1 - 2 * my_y) * flip_y
        return pltpu.make_async_remote_copy(
            src_ref=part_send.at[s], dst_ref=part_got.at[s, my_id], send_sem=send_p.at[s, p],
            recv_sem=recv_p.at[s, p], device_id=(px, py), device_id_type=MESH,
        )

    def copy_group(g):
        x, y = group_xy(g)
        return pltpu.make_async_remote_copy(
            src_ref=fin, dst_ref=gathered.at[my_group], send_sem=send_g.at[g],
            recv_sem=recv_g.at[my_group], device_id=(x, y), device_id_type=MESH,
        )

    def take_group(g):
        x, y = group_xy(g)
        return pltpu.make_async_remote_copy(
            src_ref=fin, dst_ref=gathered.at[g], send_sem=send_g.at[g],
            recv_sem=recv_g.at[g], device_id=(x, y), device_id_type=MESH,
        )

    partners = ((0, 1), (1, 0), (1, 1))

    def substep(s):
        @pl.loop(0, nx)
        def _(x):
            for c in range(3):
                parts = []
                for h in range(halves):
                    zs = slice(h * LANES, (h + 1) * LANES)
                    half = out_vel[c, x, :, zs] + 0.5 * time_step * force[c, x, h]
                    out_vel[c, x, :, zs] = half
                    moved = out_disp[c, x, :, zs] + time_step * half
                    out_disp[c, x, :, zs] = moved
                    if c == 0:
                        moved = moved + (x - mid_x).astype(jnp.float32)
                    elif c == 1:
                        rows = lax.broadcasted_iota(jnp.int32, (ny, LANES), 0)
                        moved = moved + (rows - mid_y).astype(jnp.float32)
                    parts.append(moved)
                put(c, x + 2, slice(8, 8 + ny), parts)
                for h, p in enumerate(parts):
                    edges_y[s, 0, c, x, h] = p[0:2]
                    edges_y[s, 1, c, x, h] = p[ny - 2 : ny]
                if c == 2:
                    for ref, by in ((u_pp, 2), (u_mm, -2)):
                        for h, p in enumerate(shifted(parts, by)):
                            ref[x, h] = p + float(by)

        for k, (dx, dy) in enumerate(CORNERS):
            x = 2 if dx < 0 else nx + 1
            y = 8 if dy < 0 else ny + 7
            for c in range(3):
                for h in range(halves):
                    edges_c[s, k, c, h] = u_0[c, x, h, y : y + 1, :]

        for k, d in enumerate((1, -1)):
            @pl.when(exists(d, 0))
            def _():
                copy_side(s, k, d).start()
        for k, d in enumerate((1, -1)):
            @pl.when(exists(0, d))
            def _():
                pltpu.make_async_remote_copy(
                    src_ref=edges_y.at[s, 1 - k], dst_ref=got_y.at[s, k],
                    send_sem=send_y.at[s, k], recv_sem=recv_y.at[s, k],
                    device_id=(me_x, me_y + d), device_id_type=MESH,
                ).start()
        for k, (dx, dy) in enumerate(CORNERS):
            @pl.when(exists(dx, dy))
            def _():
                copy_corner(s, k, dx, dy).start()

        for r in range(per_group):
            half = qv[r] + 0.5 * time_step * qa[r]
            qv[r] = half
            moved = qp[r] + time_step * half
            qp[r] = moved
            for c, base in enumerate(
                ((me_x * nx + mid_x).astype(jnp.float32),
                 (me_y * ny + mid_y).astype(jnp.float32), float(nz - SL))
            ):
                rel[r, c : c + 1] = moved[c : c + 1] - base

        @pl.loop(0, nx)
        def _(x):
            for c in range(3):
                for t in range(tiles):
                    tile = u_0[c, x + 2, top, 8 + 8 * t : 16 + 8 * t, :]
                    for z in range(SL):
                        col = tile[:, LANES - SL + z : LANES - SL + z + 1]
                        if c == 2:
                            col = col + float(z)
                        wide[x, c, z * tiles + t] = jnp.broadcast_to(col, (8, LANES))

        @pl.loop(0, slots)
        def _(k):
            block = targets_ref[s * slots + k]
            slot = slots_ref[s * slots + k]
            q = rel[slot]
            qs = [jnp.broadcast_to(q[c : c + 1], (8, LANES)) for c in range(3)]
            sums = [zero_tile] * 3
            for t in range(tiles):
                outs = [zero_tile] * 3
                for z in range(SL):
                    r = [wide[block, c, z * tiles + t] - qs[c] for c in range(3)]
                    sq = r[0] * r[0] + r[1] * r[1] + r[2] * r[2]
                    w = contact_stiffness * jnp.exp(sq * (-1.0 / contact_width))
                    for c in range(3):
                        pulled = w * r[c]
                        sums[c] = sums[c] + pulled
                        total = jnp.sum(pulled, axis=1, keepdims=True)
                        outs[c] = jnp.where(lane == LANES - SL + z, total, outs[c])
                for c in range(3):
                    slot_point[k, c, t * 8 : t * 8 + 8, :] = outs[c]
            for c in range(3):
                slot_part[k, c] = sums[c]

        for g in range(per_group):
            for c in range(3):
                total = zero_tile
                for x in range(nx):
                    total = total + slot_part[inverse_ref[(s * nx + x) * per_group + g], c]
                total = -jnp.sum(total, axis=0, keepdims=True)
                part_send[s, g, c : c + 1] = total
                part_got[s, my_id, g, c : c + 1] = total
        for p, (fx, fy) in enumerate(partners):
            copy_part(s, p, fx, fy).start()

        for k, d in enumerate((-1, 1)):
            @pl.when(exists(d, 0))
            def _():
                pltpu.make_async_remote_copy(
                    src_ref=got_x.at[s, k], dst_ref=got_x.at[s, k], send_sem=send_x.at[s, k],
                    recv_sem=recv_x.at[s, k], device_id=(me_x + d, me_y), device_id_type=MESH,
                ).wait_recv()
                for layer in range(2):
                    x = layer if d < 0 else nx + 2 + layer
                    near = layer == (1 if d < 0 else 0)
                    for c in range(3):
                        parts = [got_x[s, k, c, layer, h] for h in range(halves)]
                        if c == 0:
                            parts = [p + float(d * nx) for p in parts]
                        put(c, x, slice(8, 8 + ny), parts, near)
        for k, d in enumerate((-1, 1)):
            @pl.when(exists(0, d))
            def _():
                pltpu.make_async_remote_copy(
                    src_ref=got_y.at[s, k], dst_ref=got_y.at[s, k], send_sem=send_y.at[s, k],
                    recv_sem=recv_y.at[s, k], device_id=(me_x, me_y + d), device_id_type=MESH,
                ).wait_recv()

                @pl.loop(0, nx)
                def _(x):
                    for c in range(3):
                        parts = [got_y[s, k, c, x, h] for h in range(halves)]
                        if c == 1:
                            parts = [p + float(d * ny) for p in parts]
                        y = 6 if d < 0 else ny + 8
                        put(c, x + 2, slice(y, y + 2), parts)
        for k, (dx, dy) in enumerate(CORNERS):
            j = CORNERS.index((-dx, -dy))

            @pl.when(exists(dx, dy))
            def _():
                pltpu.make_async_remote_copy(
                    src_ref=got_c.at[s, j], dst_ref=got_c.at[s, j], send_sem=send_c.at[s, j],
                    recv_sem=recv_c.at[s, j], device_id=(me_x + dx, me_y + dy),
                    device_id_type=MESH,
                ).wait_recv()
                x = 1 if dx < 0 else nx + 2
                y = 7 if dy < 0 else ny + 8
                for c in range(3):
                    parts = [got_c[s, j, c, h] for h in range(halves)]
                    if c == 0:
                        parts = [p + float(dx * nx) for p in parts]
                    if c == 1:
                        parts = [p + float(dy * ny) for p in parts]
                    put(c, x, slice(y, y + 1), parts)

        @pl.loop(0, nx)
        def _(x):
            for h in range(halves):
                for t in range(tiles):
                    rows = slice(8 * t, 8 * t + 8)
                    own = [u_0[c, x + 2, h, 8 + 8 * t : 16 + 8 * t, :] for c in range(3)]
                    total = [None, None, None]
                    for n, (dx, dy, dz) in enumerate(OFFSETS):
                        length = math.sqrt(dx * dx + dy * dy + dz * dz)
                        y0 = 8 + 8 * t + dy
                        if abs(dz) == 2:
                            by = 2 if dz > 0 else -2
                            near = [
                                shifted([u_0[c, x + 2, i, y0 : y0 + 8, :] for i in range(halves)], by)[h]
                                for c in range(2)
                            ] + [(u_pp if dz > 0 else u_mm)[x, h, rows, :]]
                        else:
                            ref = {0: u_0, 1: u_p, -1: u_m}[dz]
                            near = [ref[c, x + 2 + dx, h, y0 : y0 + 8, :] for c in range(3)]
                        d = [near[c] - own[c] for c in range(3)]
                        q = d[0] * d[0] + d[1] * d[1] + d[2] * d[2]
                        root = q * lax.rsqrt(jnp.maximum(q, tiny))
                        coefficient = (root - length) * factors[n, x, h, rows, :]
                        for c, e in enumerate((dx, dy, dz)):
                            if e:
                                if total[c] is None:
                                    total[c] = coefficient if e > 0 else -coefficient
                                elif e > 0:
                                    total[c] = total[c] + coefficient
                                else:
                                    total[c] = total[c] - coefficient
                    zs = slice(h * LANES, (h + 1) * LANES)
                    for c in range(3):
                        f = total[c]
                        if h == top:
                            for g in range(per_group):
                                f = f + slot_point[inverse_ref[(s * nx + x) * per_group + g], c, rows, :]
                        force[c, x, h, rows, :] = f
                        out_vel[c, x, rows, zs] = out_vel[c, x, rows, zs] + 0.5 * time_step * f

        for p, (fx, fy) in enumerate(partners):
            ix = my_x + (1 - 2 * my_x) * fx
            iy = my_y + (1 - 2 * my_y) * fy
            pltpu.make_async_remote_copy(
                src_ref=part_send.at[s], dst_ref=part_got.at[s, ix * 2 + iy],
                send_sem=send_p.at[s, p], recv_sem=recv_p.at[s, p],
                device_id=(me_x + ix - my_x, me_y + iy - my_y), device_id_type=MESH,
            ).wait()
        for r in range(per_group):
            total = part_got[s, 0, r] + part_got[s, 1, r] + part_got[s, 2, r] + part_got[s, 3, r]
            total = inverse_mass * total
            qa[r] = total
            qv[r] = qv[r] + 0.5 * time_step * total

        for k, d in enumerate((1, -1)):
            @pl.when(exists(d, 0))
            def _():
                copy_side(s, k, d).wait_send()

            @pl.when(exists(0, d))
            def _():
                pltpu.make_async_remote_copy(
                    src_ref=edges_y.at[s, 1 - k], dst_ref=got_y.at[s, k],
                    send_sem=send_y.at[s, k], recv_sem=recv_y.at[s, k],
                    device_id=(me_x, me_y + d), device_id_type=MESH,
                ).wait_send()
        for k, (dx, dy) in enumerate(CORNERS):
            @pl.when(exists(dx, dy))
            def _():
                copy_corner(s, k, dx, dy).wait_send()

    @pl.loop(0, subs)
    def _(s):
        substep(s)

    for r in range(per_group):
        for i, ref in enumerate((qp, qv)):
            fin[r, i] = ref[r]
            gathered[my_group, r, i] = ref[r]

    @pl.loop(0, groups)
    def _(g):
        @pl.when(g != my_group)
        def _():
            copy_group(g).start()

    @pl.loop(0, groups)
    def _(g):
        @pl.when(g != my_group)
        def _():
            take_group(g).wait()

    @pl.loop(0, blocks)
    def _(b):
        where = place_ref[b]
        out_pos[b] = gathered[where // per_group, lax.rem(where, per_group), 0]
        out_pvel[b] = gathered[where // per_group, lax.rem(where, per_group), 1]


def per_device(
    slabs, splits,
    displacement, velocity, acceleration, bond_masks, proj_pos, proj_vel, proj_acc, contact_pairs
):
    _, nx, ny, nz = displacement.shape
    subs = contact_pairs.shape[0]
    slots = contact_pairs.shape[2]
    blocks = proj_pos.shape[0]
    groups = (slabs // 2) * (splits // 2)
    per_group = blocks // groups
    halves = nz // LANES
    assert nx == SB_DEV and ny * SL == PTS and ny % 8 == 0

    middle = jnp.mean(proj_pos[:, :2, :], axis=2)
    gx = jnp.clip(jnp.floor((middle[:, 0] + 0.5) / (2 * nx)).astype(jnp.int32), 0, slabs // 2 - 1)
    gy = jnp.clip(jnp.floor((middle[:, 1] + 0.5) / (2 * ny)).astype(jnp.int32), 0, splits // 2 - 1)
    group = gx * (splits // 2) + gy
    number = jnp.arange(blocks)
    rank = jnp.sum(
        ((group[:, None] == group[None, :]) & (number[None, :] < number[:, None])).astype(jnp.int32),
        axis=1,
    )
    place = jnp.minimum(rank, per_group - 1) + group * per_group
    my_group = (lax.axis_index("slab") // 2) * (splits // 2) + lax.axis_index("split") // 2
    wanted = my_group * per_group + jnp.arange(per_group)
    mine = jnp.max(jnp.where(place[None, :] == wanted[:, None], number[None, :], 0), axis=1)
    targets = contact_pairs[:, 0]
    chosen = contact_pairs[:, 1]
    slot = jnp.max(
        jnp.where(chosen[:, :, None] == mine[None, None, :], jnp.arange(per_group), 0), axis=2
    )
    hit = (
        (targets[:, None, None, :] == jnp.arange(nx)[None, :, None, None])
        & (chosen[:, None, None, :] == mine[None, None, :, None])
    )
    inverse = jnp.min(jnp.where(hit, jnp.arange(slots), slots), axis=3)

    dims = (subs, nx, ny, nz, slabs, splits, per_group, blocks)
    f32 = jnp.float32
    smem = pl.BlockSpec(memory_space=pltpu.SMEM)
    vmem = pl.BlockSpec(memory_space=pltpu.VMEM)
    padded = (3, nx + 4, halves, ny + 16, LANES)
    dma = pltpu.SemaphoreType.DMA
    scratch = [
        pltpu.VMEM(padded, f32),
        pltpu.VMEM(padded, f32),
        pltpu.VMEM(padded, f32),
        pltpu.VMEM((nx, halves, ny, LANES), f32),
        pltpu.VMEM((nx, halves, ny, LANES), f32),
        pltpu.VMEM((3, nx, halves, ny, LANES), f32),
        pltpu.VMEM((32, nx, halves, ny, LANES), f32),
        pltpu.VMEM((subs, 2, 3, nx, halves, 2, LANES), f32),
        pltpu.VMEM((subs, 4, 3, halves, 1, LANES), f32),
        pltpu.VMEM((subs, 2, 3, 2, halves, ny, LANES), f32),
        pltpu.VMEM((subs, 2, 3, nx, halves, 2, LANES), f32),
        pltpu.VMEM((subs, 4, 3, halves, 1, LANES), f32),
        pltpu.VMEM((nx, 3, ny // 8 * SL, 8, LANES), f32),
        pltpu.VMEM((slots + 1, 3, ny, LANES), f32),
        pltpu.VMEM((slots + 1, 3, 8, LANES), f32),
        pltpu.VMEM((per_group, 3, PTS), f32),
        pltpu.VMEM((per_group, 3, PTS), f32),
        pltpu.VMEM((per_group, 3, PTS), f32),
        pltpu.VMEM((per_group, 3, PTS), f32),
        pltpu.VMEM((subs, per_group, 3, PTS), f32),
        pltpu.VMEM((subs, 4, per_group, 3, PTS), f32),
        pltpu.VMEM((per_group, 2, 3, PTS), f32),
        pltpu.VMEM((groups, per_group, 2, 3, PTS), f32),
        dma((subs, 2)), dma((subs, 2)), dma((subs, 2)), dma((subs, 2)),
        dma((subs, 4)), dma((subs, 4)), dma((subs, 3)), dma((subs, 3)),
        dma((groups,)), dma((groups,)),
    ]
    return pl.pallas_call(
        functools.partial(kernel, dims),
        out_shape=(
            jax.ShapeDtypeStruct(displacement.shape, f32),
            jax.ShapeDtypeStruct(displacement.shape, f32),
            jax.ShapeDtypeStruct(proj_pos.shape, f32),
            jax.ShapeDtypeStruct(proj_pos.shape, f32),
        ),
        in_specs=[smem] * 5 + [vmem] * 7,
        out_specs=(vmem,) * 4,
        scratch_shapes=scratch,
        compiler_params=pltpu.CompilerParams(
            collective_id=0, has_side_effects=True, vmem_limit_bytes=60 * 1024 * 1024
        ),
    )(
        targets.reshape(-1), slot.reshape(-1), inverse.reshape(-1), mine, place,
        displacement, velocity, acceleration, bond_masks, proj_pos, proj_vel, proj_acc,
    )


def solution(mesh):
    cells = P(None, "slab", "split", None)
    return jax.shard_map(
        functools.partial(per_device, mesh.shape["slab"], mesh.shape["split"]),
        mesh=mesh,
        in_specs=(cells, cells, cells, cells, P(), P(), P(), P(None, None, ("slab", "split"))),
        out_specs=(cells, cells, P(), P()),
        check_vma=False,
    )
```

time: 285 us -> 61.8 us (0.22)
  the two profiles are of different devices: /device:TPU:4 before, /device:TPU:0 now
where the time goes in v1:
time: 61.8 us; the launch traced here: 61.5 us
  Pallas kernels  49.5 us (80%)
  local copies, waits for them, and re-layouts  10.4 us (17%)
  other arithmetic  0.94 us (2%)
  between operations  0.73 us (1%)
    pallas_call x1, Pallas kernels, per_device(): pl.pallas_call(functools.partial(kernel, dims), out_shape=(jax.ShapeDtype...  49.5 us
    unnamed x22, local copies, waits for them, and re-layouts  6.33 us
    pallas_call x2, local copies, waits for them, and re-layouts, per_device(): pl.pallas_call(functools.partial(kernel, dims), out_shape=(jax.ShapeDtype...  2.12 us

profile of v1, /device:TPU:0, one launch (start us, length us, event | category | flops | bytes accessed | tf_op | source)
XLA Modules:
  0.0 61.5 jit_solution(13865230868455685246)
XLA Ops:
  0.6 0.0 copy-start.1
  0.7 0.8 %copy-done.1 = f32[32,3,128]{2,0,1:T(8,128)S(1)} copy-done((f32[32,3,128]{2,0,1:T(8,128)S(1)}, f32[32,3,128]{2,0,1:T(8,128)}, u32[]{:S(2)}) %copy-start.1) | copy-done | bytes 49176
  1.4 0.0 copy-start.6
  1.4 0.1 slice_reduce_fusion
  1.5 0.0 copy-start.3
  1.6 0.2 convert_reduce_fusion
  1.8 0.0 copy-start.7
  1.8 0.2 select_reduce_fusion.2.mine_ref
  2.0 0.4 copy-done.7
  2.4 0.0 copy-done.6
  2.4 0.0 copy-start.5
  2.4 0.6 reshape_squeeze.3.targets_ref
  3.0 0.1 broadcast_compare_fusion
  3.1 0.0 copy-done.5
  3.1 0.1 select_reduce_fusion.1
  3.1 0.6 reshape.79.slots_ref
  3.7 0.3 select_reduce_fusion
  4.0 0.1 copy.22
  4.1 0.6 %reshape.80.inverse_ref = s32[96]{0:T(128)} reshape(s32[3,8,4]{2,1,0:T(8,128)S(1)} %copy.22) | data formatting | bytes 768 | tf_op jit(solution)/shard_map/reshape | solution.py:562
  4.8 0.0 copy-done.3
  4.8 0.7 %copy.24.qvel_ref = f32[32,3,128]{2,1,0:T(4,128)} copy(f32[32,3,128]{2,0,1:T(8,128)S(1)} %copy-done.3) | data formatting | bytes 98304 | tf_op args[5]
  5.4 0.1 copy-done.4
  5.6 0.7 %copy.25.qacc_ref = f32[32,3,128]{2,1,0:T(4,128)} copy(f32[32,3,128]{2,0,1:T(8,128)S(1)} %copy-done.4) | data formatting | bytes 98304 | tf_op args[6]
  6.2 0.7 %copy.23.qpos_ref = f32[32,3,128]{2,1,0:T(4,128)} copy(f32[32,3,128]{2,0,1:T(8,128)S(1)} %copy-done.1) | data formatting | bytes 98304 | tf_op args[4]
  6.9 49.5 %shard_map.111 = (f32[3,8,32,256]{3,2,1,0:T(8,128)}, f32[3,8,32,256]{3,2,1,0:T(8,128)}, f32[32,3,128]{2,1,0:T(4,128)}, f32[32,3,128]{2,1,0:T(4,128)}) custom-call(s32[48]{0:T(128)} %reshape_squeeze.3.targets_ref, s32[48]{0:T(128)} %reshape.79.slots_ref, s32[96]{0:T(128)} %reshape.80.inverse_ref, s32[4]{0:T(128)} %copy-done.5, s32[32]{0:T(128)} %copy-done.7, ...), custom_call_target="tpu_custom_call" | custom-call | tf_op jit(solution)/shard_map/pallas_call | solution.py:547
  56.4 0.0 copy-start.2
  56.4 1.5 %copy.26 = f32[32,3,128]{2,0,1:T(8,128)} copy(f32[32,3,128]{2,1,0:T(4,128)} %get-tuple-element.14) | data formatting | bytes 98304 | tf_op jit(solution)/shard_map/pallas_call | solution.py:547
  57.9 0.0 copy-done.2
  57.9 0.6 %copy.27 = f32[32,3,128]{2,0,1:T(8,128)} copy(f32[32,3,128]{2,1,0:T(4,128)S(1)} %copy-done.2) | data formatting | bytes 98304 | tf_op jit(solution)/shard_map/pallas_call | solution.py:547
  58.5 2.2 %copy.34 = f32[3,8,32,256]{3,2,1,0:T(8,128)} copy(f32[3,8,32,256]{3,2,1,0:T(8,128)} %get-tuple-element.25) | data formatting | bytes 1572864
  60.6 0.0 copy-done
  60.6 0.9 %copy.35 = f32[3,8,32,256]{3,2,1,0:T(8,128)} copy(f32[3,8,32,256]{3,2,1,0:T(8,128)S(1)} %copy-done) | data formatting | bytes 1572864
  (9 shorter events, 0.1 us)
Async XLA Ops:
  0.6 0.8 %copy-start.1 = (f32[32,3,128]{2,0,1:T(8,128)S(1)}, f32[32,3,128]{2,0,1:T(8,128)}, u32[]{:S(2)}) copy-start(f32[32,3,128]{2,0,1:T(8,128)} %param.12) | copy-start | bytes 147460
  1.4 0.9 %copy-start.6 = (s32[3,2,16]{2,1,0:T(2,128)S(1)}, s32[3,2,16]{2,1,0:T(2,128)}, u32[]{:S(2)}) copy-start(s32[3,2,16]{2,1,0:T(2,128)} %param.15) | copy-start | bytes 1156
  1.5 3.3 %copy-start.3 = (f32[32,3,128]{2,0,1:T(8,128)S(1)}, f32[32,3,128]{2,0,1:T(8,128)}, u32[]{:S(2)}) copy-start(f32[32,3,128]{2,0,1:T(8,128)} %param.13) | copy-start | bytes 147460
  1.8 0.6 copy-start.7
  2.4 0.7 %copy-start.5 = (s32[4]{0:T(128)}, s32[4]{0:T(128)S(1)}, u32[]{:S(2)}) copy-start(s32[4]{0:T(128)S(1)} %select_reduce_fusion.2.mine_ref) | copy-start | bytes 52
  4.8 0.8 %copy-start.4 = (f32[32,3,128]{2,0,1:T(8,128)S(1)}, f32[32,3,128]{2,0,1:T(8,128)}, u32[]{:S(2)}) copy-start(f32[32,3,128]{2,0,1:T(8,128)} %param.14) | copy-start | bytes 147460
  56.4 1.5 %copy-start.2 = (f32[32,3,128]{2,1,0:T(4,128)S(1)}, f32[32,3,128]{2,1,0:T(4,128)}, u32[]{:S(2)}) copy-start(f32[32,3,128]{2,1,0:T(4,128)} %get-tuple-element.15) | copy-start | bytes 147460
  58.5 2.2 %copy-start = (f32[3,8,32,256]{3,2,1,0:T(8,128)S(1)}, f32[3,8,32,256]{3,2,1,0:T(8,128)}, u32[]{:S(2)}) copy-start(f32[3,8,32,256]{3,2,1,0:T(8,128)} %get-tuple-element.26) | copy-start | bytes 2359300

commit v2 on v1

--- a/solution.py
+++ b/solution.py
@@ -41,9 +41,9 @@
 def kernel(
     dims,
     targets_ref, slots_ref, inverse_ref, mine_ref, place_ref,
-    disp_ref, vel_ref, acc_ref, mask_ref, qpos_ref, qvel_ref, qacc_ref,
+    disp_hbm, vel_hbm, acc_hbm, mask_hbm, qpos_ref, qvel_ref, qacc_ref,
     out_disp, out_vel, out_pos, out_pvel,
-    u_0, u_p, u_m, u_pp, u_mm, force, factors, edges_y, edges_c,
+    u_0, u_p, u_m, u_pp, u_mm, force, still, mask_ref, in_sem, factors, edges_y, edges_c,
     got_x, got_y, got_c, wide, slot_point, slot_part, qp, qv, qa, rel,
     part_send, part_got, fin, gathered,
     send_x, recv_x, send_y, recv_y, send_c, recv_c, send_p, recv_p, send_g, recv_g,
@@ -51,7 +51,7 @@
     subs, nx, ny, nz, slabs, splits, per_group, blocks = dims
     halves = nz // LANES
     tiles = ny // 8
-    slots = slots_ref.shape[0] // subs
+    slots = slots_ref.shape[1]
     top = halves - 1
     me_x = lax.axis_index("slab")
     me_y = lax.axis_index("split")
@@ -70,6 +70,15 @@
                 ok = cond if ok is None else ok & cond
         return ok
 
+    loads = [
+        pltpu.make_async_copy(src, dst, in_sem.at[i])
+        for i, (src, dst) in enumerate(
+            ((mask_hbm, mask_ref), (acc_hbm, force), (vel_hbm, out_vel), (disp_hbm, out_disp))
+        )
+    ]
+    for load in loads:
+        load.start()
+
     barrier = pltpu.get_barrier_semaphore()
 
     def greet(x, y):
@@ -104,6 +113,8 @@
                 for h in range(halves):
                     ref[c, x, h, 0:8, :] = zero_tile
                     ref[c, x, h, ny + 8 : ny + 16, :] = zero_tile
+
+    loads[0].wait()
 
     @pl.loop(0, nx)
     def _(x):
@@ -124,26 +135,32 @@
                     mask_ref[w, x, t * 8 : t * 8 + 8, h * LANES : (h + 1) * LANES]
                     for w in range(4)
                 ]
+                rest = [[zero_tile] * 3 for _ in range(4)]
                 for n, (dx, dy, dz) in enumerate(OFFSETS):
                     squared = dx * dx + dy * dy + dz * dz
                     scale = bond_stiffness / squared
                     if squared == 4:
                         scale = scale * 2.0
                     ok = ((words[n // 8] & (1 << (n % 8))) != 0) & ok_y[dy] & ok_z[dz]
-                    factors[n, x, h, t * 8 : t * 8 + 8, :] = jnp.where(
-                        ok, scale * ok_x[dx], 0.0
+                    factor = jnp.where(ok, scale * ok_x[dx], 0.0)
+                    factors[n, x, h, t * 8 : t * 8 + 8, :] = factor
+                    kind = squared - 1
+                    for c, e in enumerate((dx, dy, dz)):
+                        if e > 0:
+                            rest[kind][c] = rest[kind][c] + factor
+                        elif e:
+                            rest[kind][c] = rest[kind][c] - factor
+                for c in range(3):
+                    still[c, x, t * 8 : t * 8 + 8, h * LANES : (h + 1) * LANES] = (
+                        rest[0][c] + math.sqrt(2.0) * rest[1][c]
+                        + math.sqrt(3.0) * rest[2][c] + 2.0 * rest[3][c]
                     )
+
+    for r in range(per_group):
         for c in range(3):
-            for h in range(halves):
-                zs = slice(h * LANES, (h + 1) * LANES)
-                out_vel[c, x, :, zs] = vel_ref[c, x, :, zs]
-                out_disp[c, x, :, zs] = disp_ref[c, x, :, zs]
-                force[c, x, h] = acc_ref[c, x, :, zs]
-
-    for r in range(per_group):
-        qp[r] = qpos_ref[mine_ref[r]]
-        qv[r] = qvel_ref[mine_ref[r]]
-        qa[r] = qacc_ref[mine_ref[r]]
+            qp[r, c : c + 1] = qpos_ref[c, pl.ds(mine_ref[r], 1)]
+            qv[r, c : c + 1] = qvel_ref[c, pl.ds(mine_ref[r], 1)]
+            qa[r, c : c + 1] = qacc_ref[c, pl.ds(mine_ref[r], 1)]
     slot_point[slots] = jnp.zeros(slot_point.shape[1:], jnp.float32)
     slot_part[slots] = jnp.zeros(slot_part.shape[1:], jnp.float32)
 
@@ -151,6 +168,8 @@
     for dx, dy in SIDES + CORNERS:
         count = count + jnp.where(exists(dx, dy), 1, 0)
     pl.semaphore_wait(barrier, count)
+    for load in loads[1:]:
+        load.wait()
 
     def shifted(parts, by):
         rows = parts[0].shape[0]
@@ -181,12 +200,6 @@
             recv_sem=recv_x.at[s, k], device_id=(me_x + dx, me_y), device_id_type=MESH,
         )
 
-    def copy_edge(s, k, dy):
-        return pltpu.make_async_remote_copy(
-            src_ref=edges_y.at[s, k], dst_ref=got_y.at[s, k], send_sem=send_y.at[s, k],
-            recv_sem=recv_y.at[s, k], device_id=(me_x, me_y + dy), device_id_type=MESH,
-        )
-
     def copy_corner(s, k, dx, dy):
         return pltpu.make_async_remote_copy(
             src_ref=edges_c.at[s, k], dst_ref=got_c.at[s, k], send_sem=send_c.at[s, k],
@@ -218,13 +231,13 @@
     partners = ((0, 1), (1, 0), (1, 1))
 
     def substep(s):
-        @pl.loop(0, nx)
+        @pl.loop(0, nx, unroll=2)
         def _(x):
             for c in range(3):
                 parts = []
                 for h in range(halves):
                     zs = slice(h * LANES, (h + 1) * LANES)
-                    half = out_vel[c, x, :, zs] + 0.5 * time_step * force[c, x, h]
+                    half = out_vel[c, x, :, zs] + 0.5 * time_step * force[c, x, :, zs]
                     out_vel[c, x, :, zs] = half
                     moved = out_disp[c, x, :, zs] + time_step * half
                     out_disp[c, x, :, zs] = moved
@@ -251,10 +264,6 @@
                     edges_c[s, k, c, h] = u_0[c, x, h, y : y + 1, :]
 
         for k, d in enumerate((1, -1)):
-            @pl.when(exists(d, 0))
-            def _():
-                copy_side(s, k, d).start()
-        for k, d in enumerate((1, -1)):
             @pl.when(exists(0, d))
             def _():
                 pltpu.make_async_remote_copy(
@@ -266,6 +275,11 @@
             @pl.when(exists(dx, dy))
             def _():
                 copy_corner(s, k, dx, dy).start()
+
+        for k, d in enumerate((1, -1)):
+            @pl.when(exists(d, 0))
+            def _():
+                copy_side(s, k, d).start()
 
         for r in range(per_group):
             half = qv[r] + 0.5 * time_step * qa[r]
@@ -278,7 +292,7 @@
             ):
                 rel[r, c : c + 1] = moved[c : c + 1] - base
 
-        @pl.loop(0, nx)
+        @pl.loop(0, nx, unroll=4)
         def _(x):
             for c in range(3):
                 for t in range(tiles):
@@ -289,10 +303,10 @@
                             col = col + float(z)
                         wide[x, c, z * tiles + t] = jnp.broadcast_to(col, (8, LANES))
 
-        @pl.loop(0, slots)
+        @pl.loop(0, slots, unroll=4)
         def _(k):
-            block = targets_ref[s * slots + k]
-            slot = slots_ref[s * slots + k]
+            block = targets_ref[s, k]
+            slot = slots_ref[s, k]
             q = rel[slot]
             qs = [jnp.broadcast_to(q[c : c + 1], (8, LANES)) for c in range(3)]
             sums = [zero_tile] * 3
@@ -316,12 +330,70 @@
             for c in range(3):
                 total = zero_tile
                 for x in range(nx):
-                    total = total + slot_part[inverse_ref[(s * nx + x) * per_group + g], c]
+                    total = total + slot_part[inverse_ref[s, x * per_group + g], c]
                 total = -jnp.sum(total, axis=0, keepdims=True)
                 part_send[s, g, c : c + 1] = total
                 part_got[s, my_id, g, c : c + 1] = total
         for p, (fx, fy) in enumerate(partners):
             copy_part(s, p, fx, fy).start()
+
+        for k, d in enumerate((-1, 1)):
+            @pl.when(exists(0, d))
+            def _():
+                pltpu.make_async_remote_copy(
+                    src_ref=got_y.at[s, k], dst_ref=got_y.at[s, k], send_sem=send_y.at[s, k],
+                    recv_sem=recv_y.at[s, k], device_id=(me_x, me_y + d), device_id_type=MESH,
+                ).wait_recv()
+
+                @pl.loop(0, nx)
+                def _(x):
+                    for c in range(3):
+                        parts = [got_y[s, k, c, x, h] for h in range(halves)]
+                        if c == 1:
+                            parts = [p + float(d * ny) for p in parts]
+                        y = 6 if d < 0 else ny + 8
+                        put(c, x + 2, slice(y, y + 2), parts)
+        def bond_layer(x):
+            for h in range(halves):
+                for t in range(tiles):
+                    rows = slice(8 * t, 8 * t + 8)
+                    own = [u_0[c, x + 2, h, 8 + 8 * t : 16 + 8 * t, :] for c in range(3)]
+                    total = [None, None, None]
+                    for n, (dx, dy, dz) in enumerate(OFFSETS):
+                        y0 = 8 + 8 * t + dy
+                        if abs(dz) == 2:
+                            by = 2 if dz > 0 else -2
+                            near = [
+                                shifted([u_0[c, x + 2, i, y0 : y0 + 8, :] for i in range(halves)], by)[h]
+                                for c in range(2)
+                            ] + [(u_pp if dz > 0 else u_mm)[x, h, rows, :]]
+                        else:
+                            ref = {0: u_0, 1: u_p, -1: u_m}[dz]
+                            near = [ref[c, x + 2 + dx, h, y0 : y0 + 8, :] for c in range(3)]
+                        d = [near[c] - own[c] for c in range(3)]
+                        q = d[0] * d[0] + d[1] * d[1] + d[2] * d[2]
+                        root = q * lax.rsqrt(jnp.maximum(q, tiny))
+                        coefficient = root * factors[n, x, h, rows, :]
+                        for c, e in enumerate((dx, dy, dz)):
+                            if e:
+                                if total[c] is None:
+                                    total[c] = coefficient if e > 0 else -coefficient
+                                elif e > 0:
+                                    total[c] = total[c] + coefficient
+                                else:
+                                    total[c] = total[c] - coefficient
+                    zs = slice(h * LANES, (h + 1) * LANES)
+                    for c in range(3):
+                        f = total[c] - still[c, x, rows, zs]
+                        if h == top:
+                            for g in range(per_group):
+                                f = f + slot_point[inverse_ref[s, x * per_group + g], c, rows, :]
+                        force[c, x, rows, zs] = f
+                        out_vel[c, x, rows, zs] = out_vel[c, x, rows, zs] + 0.5 * time_step * f
+
+        @pl.loop(0, nx // 2)
+        def _(i):
+            bond_layer(i + nx // 4)
 
         for k, d in enumerate((-1, 1)):
             @pl.when(exists(d, 0))
@@ -338,22 +410,6 @@
                         if c == 0:
                             parts = [p + float(d * nx) for p in parts]
                         put(c, x, slice(8, 8 + ny), parts, near)
-        for k, d in enumerate((-1, 1)):
-            @pl.when(exists(0, d))
-            def _():
-                pltpu.make_async_remote_copy(
-                    src_ref=got_y.at[s, k], dst_ref=got_y.at[s, k], send_sem=send_y.at[s, k],
-                    recv_sem=recv_y.at[s, k], device_id=(me_x, me_y + d), device_id_type=MESH,
-                ).wait_recv()
-
-                @pl.loop(0, nx)
-                def _(x):
-                    for c in range(3):
-                        parts = [got_y[s, k, c, x, h] for h in range(halves)]
-                        if c == 1:
-                            parts = [p + float(d * ny) for p in parts]
-                        y = 6 if d < 0 else ny + 8
-                        put(c, x + 2, slice(y, y + 2), parts)
         for k, (dx, dy) in enumerate(CORNERS):
             j = CORNERS.index((-dx, -dy))
 
@@ -374,45 +430,9 @@
                         parts = [p + float(dy * ny) for p in parts]
                     put(c, x, slice(y, y + 1), parts)
 
-        @pl.loop(0, nx)
-        def _(x):
-            for h in range(halves):
-                for t in range(tiles):
-                    rows = slice(8 * t, 8 * t + 8)
-                    own = [u_0[c, x + 2, h, 8 + 8 * t : 16 + 8 * t, :] for c in range(3)]
-                    total = [None, None, None]
-                    for n, (dx, dy, dz) in enumerate(OFFSETS):
-                        length = math.sqrt(dx * dx + dy * dy + dz * dz)
-                        y0 = 8 + 8 * t + dy
-                        if abs(dz) == 2:
-                            by = 2 if dz > 0 else -2
-                            near = [
-                                shifted([u_0[c, x + 2, i, y0 : y0 + 8, :] for i in range(halves)], by)[h]
-                                for c in range(2)
-                            ] + [(u_pp if dz > 0 else u_mm)[x, h, rows, :]]
-                        else:
-                            ref = {0: u_0, 1: u_p, -1: u_m}[dz]
-                            near = [ref[c, x + 2 + dx, h, y0 : y0 + 8, :] for c in range(3)]
-                        d = [near[c] - own[c] for c in range(3)]
-                        q = d[0] * d[0] + d[1] * d[1] + d[2] * d[2]
-                        root = q * lax.rsqrt(jnp.maximum(q, tiny))
-                        coefficient = (root - length) * factors[n, x, h, rows, :]
-                        for c, e in enumerate((dx, dy, dz)):
-                            if e:
-                                if total[c] is None:
-                                    total[c] = coefficient if e > 0 else -coefficient
-                                elif e > 0:
-                                    total[c] = total[c] + coefficient
-                                else:
-                                    total[c] = total[c] - coefficient
-                    zs = slice(h * LANES, (h + 1) * LANES)
-                    for c in range(3):
-                        f = total[c]
-                        if h == top:
-                            for g in range(per_group):
-                                f = f + slot_point[inverse_ref[(s * nx + x) * per_group + g], c, rows, :]
-                        force[c, x, h, rows, :] = f
-                        out_vel[c, x, rows, zs] = out_vel[c, x, rows, zs] + 0.5 * time_step * f
+        @pl.loop(0, nx // 2)
+        def _(i):
+            bond_layer(jnp.where(i < nx // 4, i, i + nx // 2))
 
         for p, (fx, fy) in enumerate(partners):
             ix = my_x + (1 - 2 * my_x) * fx
@@ -469,8 +489,27 @@
     @pl.loop(0, blocks)
     def _(b):
         where = place_ref[b]
-        out_pos[b] = gathered[where // per_group, lax.rem(where, per_group), 0]
-        out_pvel[b] = gathered[where // per_group, lax.rem(where, per_group), 1]
+        both = [gathered[where // per_group, lax.rem(where, per_group), i] for i in range(2)]
+        for c in range(3):
+            out_pos[c, pl.ds(b, 1)] = both[0][c : c + 1]
+            out_pvel[c, pl.ds(b, 1)] = both[1][c : c + 1]
+
+
+def finish_kernel(moved_ref, speed_ref, out_moved, out_speed):
+    out_moved[...] = moved_ref[...]
+    out_speed[...] = speed_ref[...]
+
+
+def finish(moved, speed):
+    block = pl.BlockSpec((1,) + moved.shape[1:], lambda c: (c, 0, 0, 0))
+    return pl.pallas_call(
+        finish_kernel,
+        grid=(moved.shape[0],),
+        out_shape=(jax.ShapeDtypeStruct(moved.shape, moved.dtype),) * 2,
+        in_specs=[block] * 2,
+        out_specs=(block,) * 2,
+        compiler_params=pltpu.CompilerParams(vmem_limit_bytes=16 * 1024 * 1024),
+    )(moved, speed)
 
 
 def per_device(
@@ -504,11 +543,11 @@
     slot = jnp.max(
         jnp.where(chosen[:, :, None] == mine[None, None, :], jnp.arange(per_group), 0), axis=2
     )
-    hit = (
-        (targets[:, None, None, :] == jnp.arange(nx)[None, :, None, None])
-        & (chosen[:, None, None, :] == mine[None, None, :, None])
+    pairs = jnp.arange(nx * per_group)
+    hit = (targets[:, None, :] == (pairs // per_group)[None, :, None]) & (
+        chosen[:, None, :] == jnp.tile(mine, nx)[None, :, None]
     )
-    inverse = jnp.min(jnp.where(hit, jnp.arange(slots), slots), axis=3)
+    inverse = jnp.min(jnp.where(hit, jnp.arange(slots), slots), axis=2)
 
     dims = (subs, nx, ny, nz, slabs, splits, per_group, blocks)
     f32 = jnp.float32
@@ -522,7 +561,10 @@
         pltpu.VMEM(padded, f32),
         pltpu.VMEM((nx, halves, ny, LANES), f32),
         pltpu.VMEM((nx, halves, ny, LANES), f32),
-        pltpu.VMEM((3, nx, halves, ny, LANES), f32),
+        pltpu.VMEM((3, nx, ny, nz), f32),
+        pltpu.VMEM((3, nx, ny, nz), f32),
+        pltpu.VMEM((4, nx, ny, nz), jnp.int32),
+        pltpu.SemaphoreType.DMA((4,)),
         pltpu.VMEM((32, nx, halves, ny, LANES), f32),
         pltpu.VMEM((subs, 2, 3, nx, halves, 2, LANES), f32),
         pltpu.VMEM((subs, 4, 3, halves, 1, LANES), f32),
@@ -544,24 +586,27 @@
         dma((subs, 4)), dma((subs, 4)), dma((subs, 3)), dma((subs, 3)),
         dma((groups,)), dma((groups,)),
     ]
-    return pl.pallas_call(
+    moved, speed, points, point_speed = pl.pallas_call(
         functools.partial(kernel, dims),
         out_shape=(
             jax.ShapeDtypeStruct(displacement.shape, f32),
             jax.ShapeDtypeStruct(displacement.shape, f32),
-            jax.ShapeDtypeStruct(proj_pos.shape, f32),
-            jax.ShapeDtypeStruct(proj_pos.shape, f32),
+            jax.ShapeDtypeStruct((3, blocks, PTS), f32),
+            jax.ShapeDtypeStruct((3, blocks, PTS), f32),
         ),
-        in_specs=[smem] * 5 + [vmem] * 7,
+        in_specs=[smem] * 5 + [pl.BlockSpec(memory_space=pl.ANY)] * 4 + [vmem] * 3,
         out_specs=(vmem,) * 4,
         scratch_shapes=scratch,
         compiler_params=pltpu.CompilerParams(
             collective_id=0, has_side_effects=True, vmem_limit_bytes=60 * 1024 * 1024
         ),
     )(
-        targets.reshape(-1), slot.reshape(-1), inverse.reshape(-1), mine, place,
-        displacement, velocity, acceleration, bond_masks, proj_pos, proj_vel, proj_acc,
+        targets, slot, inverse, mine, place,
+        displacement, velocity, acceleration, bond_masks,
+        jnp.moveaxis(proj_pos, 1, 0), jnp.moveaxis(proj_vel, 1, 0), jnp.moveaxis(proj_acc, 1, 0),
     )
+    moved, speed = finish(moved, speed)
+    return moved, speed, jnp.moveaxis(points, 0, 1), jnp.moveaxis(point_speed, 0, 1)
 
 
 def solution(mesh):

time: 61.8 us -> 55.5 us (0.90)
  local copies, waits for them, and re-layouts: 10.4 us -> 4.89 us
  Pallas kernels: 49.5 us -> 47.6 us
  other arithmetic: 0.94 us -> 1.84 us
    pallas_call x1, Pallas kernels: 49.5 us -> 46 us  [per_device(): pl.pallas_call(functools.partial(kernel, dims), out_shape=(jax.ShapeDtype...]
    pallas_call x2 -> x0, local copies, waits for them, and re-layouts: 2.12 us -> none  [per_device(): pl.pallas_call(functools.partial(kernel, dims), out_shape=(jax.ShapeDtype...]
    pallas_call x0 -> x1, Pallas kernels: none -> 1.65 us  [finish(): pl.pallas_call(finish_kernel, grid=(moved.shape[0],), out_shape=(jax.Shap...]
    unnamed x22 -> x21, local copies, waits for them, and re-layouts: 6.33 us -> 4.8 us
    reshape x2 -> x0, local copies, waits for them, and re-layouts: 1.24 us -> none  [the longest x1 0.64 us: per_device(): inverse.reshape(-1)]
where the time goes in v2:
time: 55.5 us; the launch traced here: 55.1 us
  Pallas kernels  47.6 us (86%)
  local copies, waits for them, and re-layouts  4.89 us (9%)
  other arithmetic  1.84 us (3%)
  between operations  0.75 us (1%)
    pallas_call x1, Pallas kernels, per_device(): pl.pallas_call(functools.partial(kernel, dims), out_shape=(jax.ShapeDtype...  46 us
    unnamed x21, local copies, waits for them, and re-layouts  4.8 us
    pallas_call x1, Pallas kernels, finish(): pl.pallas_call(finish_kernel, grid=(moved.shape[0],), out_shape=(jax.Shap...  1.65 us

profile of v2, /device:TPU:0, one launch (start us, length us, event | category | flops | bytes accessed | tf_op | source)
XLA Modules:
  0.0 55.1 jit_solution(4078282235051967213)
XLA Ops:
  0.6 0.0 copy-start.2
  0.7 0.7 %copy-done.2 = f32[32,3,128]{2,0,1:T(8,128)S(1)} copy-done((f32[32,3,128]{2,0,1:T(8,128)S(1)}, f32[32,3,128]{2,0,1:T(8,128)}, u32[]{:S(2)}) %copy-start.2) | copy-done | bytes 49176
  1.4 0.1 slice_reduce_fusion
  1.5 0.0 copy-start.7
  1.6 0.2 convert_reduce_fusion
  1.8 0.0 copy-start.8
  1.8 0.2 select_reduce_fusion.2.mine_ref
  2.0 0.3 copy-done.8
  2.3 0.0 copy-done.7
  2.3 0.0 copy-start.6
  2.3 0.0 copy-start.5
  2.3 0.7 %select_reduce_fusion.1.slots_ref = s32[3,16]{1,0:T(4,128)} fusion(s32[3,16]{1,0:T(4,128)S(1)} %get-tuple-element.18, s32[4]{0:T(128)S(1)} %select_reduce_fusion.2.mine_ref), kind=kLoop, calls=%fused_computation.5 | loop fusion | flops 528 | bytes 400 | tf_op jit(solution)/shard_map/reduce_max | solution.py:543
  3.0 0.0 copy-done.6
  3.0 0.1 eq.86
  3.1 0.0 copy-done.5
  3.1 0.7 %select_reduce_fusion.inverse_ref = s32[3,32]{1,0:T(4,128)} fusion(s32[32]{0:T(128)S(1)} %eq.86, s32[3,16]{1,0:T(4,128)S(1)} %get-tuple-element.18, s32[32]{0:T(128)S(1)} %and_select_fusion, s32[3,16]{1,0:T(4,128)S(1)} %get-tuple-element.19.targets_ref), kind=kLoop, calls=%fused_computation.1 | loop fusion | flops 7584 | bytes 1024 | tf_op jit(solution)/shard_map/reduce_min | solution.py:550
  3.8 46.0 %shard_map.111 = (f32[3,8,32,256]{3,2,1,0:T(8,128)}, f32[3,8,32,256]{3,2,1,0:T(8,128)}, f32[3,32,128]{2,1,0:T(8,128)}, f32[3,32,128]{2,1,0:T(8,128)}) custom-call(s32[3,16]{1,0:T(4,128)} %copy-done.5, s32[3,16]{1,0:T(4,128)} %select_reduce_fusion.1.slots_ref, s32[3,32]{1,0:T(4,128)} %select_reduce_fusion.inverse_ref, s32[4]{0:T(128)} %copy-done.6, ...), custom_call_target="tpu_custom_call" | custom-call | tf_op jit(solution)/shard_map/pallas_call | solution.py:589
  49.7 0.0 copy-start
  49.7 1.1 %copy-done = f32[3,8,32,256]{3,2,1,0:T(8,128)S(1)} copy-done((f32[3,8,32,256]{3,2,1,0:T(8,128)S(1)}, f32[3,8,32,256]{3,2,1,0:T(8,128)}, u32[]{:S(2)}) %copy-start) | copy-done | bytes 786456
  50.9 0.0 copy-start.1
  50.9 1.1 %copy-done.1 = f32[3,8,32,256]{3,2,1,0:T(8,128)S(1)} copy-done((f32[3,8,32,256]{3,2,1,0:T(8,128)S(1)}, f32[3,8,32,256]{3,2,1,0:T(8,128)}, u32[]{:S(2)}) %copy-start.1) | copy-done | bytes 786456
  52.0 0.0 copy-start.4
  52.0 1.6 %shard_map.112 = (f32[3,8,32,256]{3,2,1,0:T(8,128)}, f32[3,8,32,256]{3,2,1,0:T(8,128)}) custom-call(f32[3,8,32,256]{3,2,1,0:T(8,128)S(1)} %copy-done, f32[3,8,32,256]{3,2,1,0:T(8,128)S(1)} %copy-done.1), custom_call_target="tpu_custom_call" | custom-call | tf_op jit(solution)/shard_map/pallas_call | solution.py:505
  53.6 0.0 copy-done.4
  53.6 0.0 copy-start.3
  53.6 0.6 %copy.18 = f32[32,3,128]{2,0,1:T(8,128)} copy(f32[32,3,128]{2,0,1:T(8,128)S(1)} %bitcast.17) | data formatting | bytes 98304
  54.3 0.2 copy-done.3
  54.5 0.6 %copy.19 = f32[32,3,128]{2,0,1:T(8,128)} copy(f32[32,3,128]{2,0,1:T(8,128)S(1)} %bitcast.16) | data formatting | bytes 98304
  (8 shorter events, 0.1 us)
Async XLA Ops:
  0.6 0.8 %copy-start.2 = (f32[32,3,128]{2,0,1:T(8,128)S(1)}, f32[32,3,128]{2,0,1:T(8,128)}, u32[]{:S(2)}) copy-start(f32[32,3,128]{2,0,1:T(8,128)} %param.12) | copy-start | bytes 147460
  1.5 0.7 %copy-start.7 = (s32[3,2,16]{2,1,0:T(2,128)S(1)}, s32[3,2,16]{2,1,0:T(2,128)}, u32[]{:S(2)}) copy-start(s32[3,2,16]{2,1,0:T(2,128)} %param.15) | copy-start | bytes 1156
  1.8 0.5 copy-start.8
  2.3 0.7 %copy-start.6 = (s32[4]{0:T(128)}, s32[4]{0:T(128)S(1)}, u32[]{:S(2)}) copy-start(s32[4]{0:T(128)S(1)} %select_reduce_fusion.2.mine_ref) | copy-start | bytes 52
  2.3 0.8 %copy-start.5 = (s32[3,16]{1,0:T(4,128)}, s32[3,16]{1,0:T(4,128)S(1)}, u32[]{:S(2)}) copy-start(s32[3,16]{1,0:T(4,128)S(1)} %get-tuple-element.19.targets_ref) | copy-start | bytes 580
  49.7 1.1 %copy-start = (f32[3,8,32,256]{3,2,1,0:T(8,128)S(1)}, f32[3,8,32,256]{3,2,1,0:T(8,128)}, u32[]{:S(2)}) copy-start(f32[3,8,32,256]{3,2,1,0:T(8,128)} %get-tuple-element.10.moved_ref) | copy-start | bytes 2359300
  50.9 1.1 %copy-start.1 = (f32[3,8,32,256]{3,2,1,0:T(8,128)S(1)}, f32[3,8,32,256]{3,2,1,0:T(8,128)}, u32[]{:S(2)}) copy-start(f32[3,8,32,256]{3,2,1,0:T(8,128)} %get-tuple-element.11.speed_ref) | copy-start | bytes 2359300
  52.0 1.7 %copy-start.4 = (f32[3,32,128]{2,1,0:T(8,128)S(1)}, f32[3,32,128]{2,1,0:T(8,128)}, u32[]{:S(2)}) copy-start(f32[3,32,128]{2,1,0:T(8,128)} %get-tuple-element.14) | copy-start | bytes 147460
  53.6 0.8 %copy-start.3 = (f32[3,32,128]{2,1,0:T(8,128)S(1)}, f32[3,32,128]{2,1,0:T(8,128)}, u32[]{:S(2)}) copy-start(f32[3,32,128]{2,1,0:T(8,128)} %get-tuple-element.15) | copy-start | bytes 147460
